TPU v7x, 256 devices: a whole 4x4x8 slice. The times are simulated.
256 devices in a mesh: freq: 64 (over x, z_lo, y), chan: 4 (over z_hi, core).
Axes of the slice: x: 4, y: 4, z: 8 (z_hi: 2, z_lo: 4; z = z_hi * 4 + z_lo), core: 2. Of those that a mesh axis runs over, the one named last changes fastest.
Arguments:
- factor: bfloat16 [512, 2, 128, 128], P('freq', None, 'chan'), may hold values from -0.2 to 1.2, as said below
- spectrum: bfloat16 [512, 2, 128, 128], P('freq', None, 'chan'), may hold values from -2 to 5, as said below
- guess_scale: float32 [512], P('freq'), may hold values from 0.1 to 0.3
- lag_cutoff: int32 [1], replicated, may hold values from 64 to 255
Outputs:
- new_factor: float32 [512, 2, 128, 128], P('freq', None, None, 'chan')
Inputs may be any that keep to these rules, and one draw needn't show every extreme that they name: The real part of factor is the identity plus independent entries of spread about 0.35 / sqrt(128). At every frequency spectrum is Hermitian: its real part symmetric, its imaginary part antisymmetric with a zero diagonal; it is positive definite.
All inputs are finite; a program needn't handle non-finite values.
Results may differ from a plain program's by a relative error of at most 0.00105.
Values may be sent and summed in bfloat16 or wider, within the bound.
A program may use at most 64 MiB of HBM per device.

v0:
```python
import functools

import jax
import jax.numpy as jnp
import numpy as np
from jax import lax
from jax.experimental import pallas as pl
from jax.experimental.pallas import tpu as pltpu
from jax.sharding import PartitionSpec as P

ITERS = 8
MESH = pl.DeviceIdType.MESH
BF = jnp.bfloat16
F32 = jnp.float32
C = 128
PANEL = 32
FL = 8
OWN = 2
G = 64
F = 512
LAGS = 256
Z_ORDER = (4, 3, 5, 2, 6, 1, 7, 0)
XY_ORDER = (2, 1, 3, 0)


def rem(a, b):
    return lax.rem(a, jnp.int32(b))


def div(a, b):
    return lax.div(a, jnp.int32(b))


def coords():
    f = lax.axis_index("freq")
    c = lax.axis_index("chan")
    return div(f, 16), rem(f, 4), div(c, 2) * 4 + rem(div(f, 4), 4), rem(c, 2)


def place(x, y, z, k):
    return (x * 4 + rem(z, 4)) * 4 + y, div(z, 4) * 2 + k


def split(value):
    high = value.astype(BF)
    return high, (value - high.astype(F32)).astype(BF)


def embed(value):
    re, im = value[:, :C], value[:, C:]
    return jnp.concatenate([value, jnp.concatenate([-im, re], axis=1)], axis=0)


def dot(left, right):
    return jnp.dot(left, right, preferred_element_type=F32)


def dot_nt(left, right):
    return lax.dot_general(left, right, (((1,), (1,)), ((), ())), preferred_element_type=F32)


def dot_tn(left, right):
    return lax.dot_general(left, right, (((0,), (0,)), ((), ())), preferred_element_type=F32)


def dot_tt(left, right):
    return lax.dot_general(left, right, (((0,), (1,)), ((), ())), preferred_element_type=F32)


def tables():
    lag = np.arange(LAGS)[:, None]
    freq = np.arange(F)[None, :]
    angle = 2.0 * np.pi * ((lag * freq) % F) / F
    cos, sin = np.cos(angle), np.sin(angle)
    to_lag = np.concatenate([cos, sin], axis=1) / F
    to_freq = np.concatenate([cos.T, -sin.T], axis=1)

    def halves(table):
        high = table.astype(jnp.bfloat16)
        low = (table - high.astype(np.float64)).astype(jnp.bfloat16)
        return np.concatenate([high, low], axis=0)

    return halves(to_lag), halves(to_freq)


def turn(value, lane):
    ahead = pltpu.roll(value, 96, 1)
    behind = pltpu.roll(value, 32, 1)
    return jnp.where(rem(lane, 64) < 32, -ahead, behind)


def table_apply(table_ref, rows, value, lane):
    high, low = split(value)
    turn_high, turn_low = turn(value, lane), None
    turn_high, turn_low = split(turn_high)
    both = jnp.concatenate(
        [jnp.concatenate([high, low], axis=1), jnp.concatenate([turn_high, turn_low], axis=1)], axis=0
    )
    first = dot(table_ref[0:rows, :], both)
    second = dot(table_ref[rows : 2 * rows, :], jnp.concatenate([high, turn_high], axis=0))
    return first[:, :C] + first[:, C:] + second


def kernel(
    factor_ref, spectrum_ref, psi_ref, scale_ref, cutoff_ref, to_lag_hbm, to_freq_hbm, out_ref,
    spec_all, psi_all, send_f, recv_f, send_r, recv_r, to_lag, to_freq,
    stage_sem, table_sem, local_sem, spec_ss, spec_rs, psi_ss, psi_rs, relay_ss, relay_rs, fwd_ss, fwd_rs, fwd_ls, ret_ss, ret_rs, ret_ls,
):
    x, y, z, k = coords()
    me_f = lax.axis_index("freq")
    me_c = lax.axis_index("chan")
    me_lin = me_f * 4 + me_c

    on_x = [place(rem(x + i, 4), y, z, k) for i in (1, 2, 3)]
    on_y = [place(x, rem(y + i, 4), z, k) for i in (1, 2, 3)]
    on_z = [place(x, y, rem(z + i, 8), k) for i in range(1, 8)]
    sibling = place(x, y, z, 1 - k)
    across = place(x, y, rem(z + 4, 8), k)
    diagonal = place(x, y, rem(z + 4, 8), 1 - k)

    def signal(sem, peers):
        for peer in peers:
            pl.semaphore_signal(sem, inc=1, device_id=peer, device_id_type=MESH)

    barrier = pltpu.get_barrier_semaphore()
    first_peers = on_x + on_y + on_z + [sibling, diagonal]
    signal(barrier, first_peers)

    tables_in = [
        pltpu.make_async_copy(to_lag_hbm, to_lag, table_sem.at[0]),
        pltpu.make_async_copy(to_freq_hbm, to_freq, table_sem.at[1]),
    ]
    for copy in tables_in:
        copy.start()

    my_rows = pl.ds(pl.multiple_of(me_c * PANEL, PANEL), PANEL)
    own_copies = [
        pltpu.make_async_copy(factor_ref, psi_all.at[:, :, my_rows, :], local_sem.at[0]),
        pltpu.make_async_copy(spectrum_ref.at[pl.ds(OWN * me_c, OWN)], spec_all.at[:, :, my_rows, :], local_sem.at[1]),
    ]
    for copy in own_copies:
        copy.start()

    def remote(src, dst, send_sem, recv_sem, peer):
        return pltpu.make_async_remote_copy(
            src_ref=src, dst_ref=dst, send_sem=send_sem, recv_sem=recv_sem, device_id=peer, device_id_type=MESH
        )

    row = lax.broadcasted_iota(jnp.int32, (C, 2 * C), 0)
    col = lax.broadcasted_iota(jnp.int32, (C, 2 * C), 1)
    eye = (row == col).astype(F32)
    lane = lax.broadcasted_iota(jnp.int32, (G, C), 1)

    psis, rs, qs = [], [], []
    for b in range(OWN):
        psi = jnp.concatenate([psi_ref[b, 0], psi_ref[b, 1]], axis=1)
        wide = embed(psi)
        r = eye - scale_ref[OWN * me_c + b] * dot_nt(psi, jnp.concatenate([psi, jnp.concatenate([-psi[:, C:], psi[:, :C]], axis=1)], axis=0))
        psis.append(wide)
        rs.append(r)
        qs.append(eye + r)

    copies = []
    for step in range(1, ITERS):
        for b in range(OWN):
            r_high, r_low = split(rs[b])
            q_high, q_low = split(qs[b])
            square_left = jnp.concatenate([r_high, r_low, r_high], axis=1)
            e_high, e_low = embed(r_high), embed(r_low)
            right = jnp.concatenate([e_high, e_high, e_low], axis=0)
            r_next = dot(square_left, right)
            rs[b] = r_next
            n_high, n_low = split(r_next)
            en_high, en_low = embed(n_high), embed(n_low)
            qs[b] = qs[b] + dot(
                jnp.concatenate([q_high, q_low, q_high], axis=1), jnp.concatenate([en_high, en_high, en_low], axis=0)
            )
        if step == 1:
            pl.semaphore_wait(barrier, len(first_peers))
            for peer in (across, diagonal, sibling):
                copies.append(
                    remote(
                        spectrum_ref.at[pl.ds(OWN * peer[1], OWN)], spec_all.at[:, :, my_rows, :], spec_ss, spec_rs, peer
                    )
                )
                copies[-1].start()
            for peer in (across, sibling):
                i = 0 if peer is across else 1
                remote(factor_ref, psi_all.at[:, :, my_rows, :], psi_ss.at[i], psi_rs.at[i], peer).start()
            signal(stage_sem.at[0], [sibling])
        if step == 3:
            pl.semaphore_wait(stage_sem.at[0], 1)
            signal(stage_sem.at[1], on_y)
        if step == 5:
            pl.semaphore_wait(stage_sem.at[1], 3)
            signal(stage_sem.at[2], on_z)

    own_copies[1].wait()
    three = spec_all.at[:, :, pl.ds(0, 3 * PANEL), :]
    pltpu.make_async_copy(three, three, spec_rs).wait()

    for b in range(OWN):
        q_high, q_low = split(qs[b])
        zz = scale_ref[OWN * me_c + b] * dot(
            jnp.concatenate([q_high, q_low], axis=1), jnp.concatenate([psis[b], psis[b]], axis=0)
        )
        z_high, z_low = split(zz)
        spec = jnp.concatenate([spec_all[b, 0], spec_all[b, 1]], axis=1)
        u = dot(
            jnp.concatenate([spec, spec], axis=1), jnp.concatenate([embed(z_high), embed(z_low)], axis=0)
        )
        u_high, u_low = split(u)

        def upright(value):
            return jnp.concatenate([value[:, :C], -value[:, C:]], axis=0)

        zs_high, zs_low = upright(z_high), upright(z_low)
        eu_high, eu_low = embed(u_high), embed(u_low)
        mid = eye + dot_tn(
            jnp.concatenate([zs_high, zs_low, zs_high], axis=0), jnp.concatenate([eu_high, eu_high, eu_low], axis=0)
        )
        pieces = [mid[:G, :C], mid[:G, C:], mid[G:, :C], mid[G:, C:]]
        for j in range(4):
            rolled = []
            for i, piece in enumerate(pieces):
                shift = (32 * i - 32 * j) % C
                rolled.append(pltpu.roll(piece, shift, 1) if shift else piece)
            packed = jnp.where(
                lane < 64,
                jnp.where(lane < 32, rolled[0], rolled[1]),
                jnp.where(lane < 96, rolled[2], rolled[3]),
            )
            send_f[pl.ds(G * j, G), b, :] = packed

    pl.semaphore_wait(stage_sem.at[2], 7)
    mine = pltpu.make_async_copy(send_f.at[me_c * G + me_f], recv_f.at[me_lin], fwd_ls)
    mine.start()
    for dx in XY_ORDER:
        for dy in XY_ORDER:
            for dk in (1, 0):
                for dz in Z_ORDER:
                    if (dx, dy, dz, dk) == (0, 0, 0, 0):
                        continue
                    peer = place(rem(x + dx, 4), rem(y + dy, 4), rem(z + dz, 8), 1 - k if dk else k)
                    remote(send_f.at[peer[1] * G + peer[0]], recv_f.at[me_lin], fwd_ss, fwd_rs, peer).start()

    own_copies[0].wait()
    across_rows = pl.ds(pl.multiple_of(across[1] * PANEL, PANEL), PANEL)
    diagonal_rows = pl.ds(pl.multiple_of(diagonal[1] * PANEL, PANEL), PANEL)
    sibling_rows = pl.ds(pl.multiple_of(sibling[1] * PANEL, PANEL), PANEL)
    panel = psi_all.at[:, :, across_rows, :]
    pltpu.make_async_copy(panel, panel, psi_rs.at[0]).wait()
    relay = remote(panel, panel, relay_ss, relay_rs, sibling)
    relay.start()

    for copy in tables_in:
        copy.wait()
    most = recv_f.at[pl.ds(0, 4 * G - 1)]
    mine.wait()
    pltpu.make_async_copy(most, most, fwd_rs).wait()

    gathered = recv_f[...].reshape(F, C)
    lane_f = lax.broadcasted_iota(jnp.int32, (F, C), 1)
    lane_l = lax.broadcasted_iota(jnp.int32, (LAGS, C), 1)
    lag_row = lax.broadcasted_iota(jnp.int32, (LAGS, C), 0)
    keep = jnp.where(lag_row == 0, 0.5, jnp.where(lag_row <= cutoff_ref[0], 1.0, 0.0)).astype(F32)
    lags = table_apply(to_lag, LAGS, gathered, lane_f) * keep
    send_r[...] = table_apply(to_freq, F, lags, lane_l)

    me_eight = pl.ds(pl.multiple_of(me_f * FL, FL), FL)
    back = pltpu.make_async_copy(send_r.at[me_eight, :], recv_r.at[me_eight, :], ret_ls)
    back.start()
    for dx in XY_ORDER:
        for dy in XY_ORDER:
            for dz in (3, 1, 2, 0):
                if (dx, dy, dz) == (0, 0, 0):
                    continue
                other = (rem(x + dx, 4) * 4 + rem(rem(z, 4) + dz, 4)) * 4 + rem(y + dy, 4)
                eight = pl.ds(pl.multiple_of(other * FL, FL), FL)
                remote(send_r.at[eight, :], recv_r.at[me_eight, :], ret_ss, ret_rs, (other, me_c)).start()

    panel = psi_all.at[:, :, sibling_rows, :]
    pltpu.make_async_copy(panel, panel, psi_rs.at[1]).wait()
    panel = psi_all.at[:, :, diagonal_rows, :]
    pltpu.make_async_copy(panel, panel, relay_rs).wait()
    back.wait()
    most = recv_r.at[pl.ds(0, F - FL), :]
    pltpu.make_async_copy(most, most, ret_rs).wait()

    for f in range(FL):
        d = recv_r[pl.ds(f, G, stride=FL), :]
        high, low = split(d)
        stack = jnp.concatenate(
            [
                jnp.concatenate([high[:, :64], low[:, :64]], axis=1),
                jnp.concatenate([high[:, 64:], low[:, 64:]], axis=1),
            ],
            axis=0,
        )
        both = jnp.concatenate([psi_all[f, 0], psi_all[f, 1]], axis=0)
        got = dot_tt(stack, both)
        got = got[:64] + got[64:]
        out_ref[f, 0] = got[:32, :C] - got[32:, C:]
        out_ref[f, 1] = got[32:, :C] + got[:32, C:]

    for i in range(2):
        pltpu.make_async_copy(factor_ref, factor_ref, psi_ss.at[i]).wait()
    pltpu.make_async_copy(three, three, spec_ss).wait()
    relay.wait_send()
    most = send_f.at[pl.ds(0, 4 * G - 1)]
    pltpu.make_async_copy(most, most, fwd_ss).wait()
    most = send_r.at[pl.ds(0, F - FL), :]
    pltpu.make_async_copy(most, most, ret_ss).wait()


def step(factor, spectrum, guess_scale, lag_cutoff):
    to_lag, to_freq = tables()
    psi = lax.all_to_all(factor, "chan", split_axis=0, concat_axis=2, tiled=True)
    vmem = pl.BlockSpec(memory_space=pltpu.VMEM)
    smem = pl.BlockSpec(memory_space=pltpu.SMEM)
    hbm = pl.BlockSpec(memory_space=pl.ANY)
    dma = pltpu.SemaphoreType.DMA
    out = pl.pallas_call(
        kernel,
        out_shape=jax.ShapeDtypeStruct((FL, 2, PANEL, C), F32),
        in_specs=[vmem, vmem, vmem, smem, smem, hbm, hbm],
        out_specs=vmem,
        scratch_shapes=[
            pltpu.VMEM((OWN, 2, C, C), BF),
            pltpu.VMEM((FL, 2, C, C), BF),
            pltpu.VMEM((4 * G, OWN, C), F32),
            pltpu.VMEM((4 * G, OWN, C), F32),
            pltpu.VMEM((F, C), F32),
            pltpu.VMEM((F, C), F32),
            pltpu.VMEM(to_lag.shape, BF),
            pltpu.VMEM(to_freq.shape, BF),
            pltpu.SemaphoreType.REGULAR((3,)),
            dma((2,)),
            dma((2,)),
            dma, dma, dma((2,)), dma((2,)), dma, dma, dma, dma, dma, dma, dma, dma,
        ],
        compiler_params=pltpu.CompilerParams(collective_id=0, has_side_effects=True, vmem_limit_bytes=40 * 1024 * 1024),
    )(factor, spectrum, psi, guess_scale, lag_cutoff, jnp.asarray(to_lag), jnp.asarray(to_freq))
    return jnp.swapaxes(out, 2, 3)


def solution(mesh):
    in_specs = (P("freq", None, "chan", None), P("freq", None, "chan", None), P("freq"), P())
    out_specs = P("freq", None, None, "chan")
    return jax.shard_map(step, mesh=mesh, in_specs=in_specs, out_specs=out_specs, check_vma=False)
```

profile of v0, /device:TPU:1, one launch (start us, length us, event | category | flops | bytes accessed | tf_op | source)
XLA Modules:
  0.0 57.8 jit_solution(14519957372068265850)
XLA Ops:
  0.0 9.9 %all-to-all-start = ((bf16[8,2,32,128]{3,2,1,0:T(8,128)(2,1)}), bf16[8,2,32,128]{3,2,1,0:T(8,128)(2,1)S(1)}, u32[]{:S(2)}, u32[]{:S(2)}) async-start(bf16[8,2,32,128]{3,2,1,0:T(8,128)(2,1)} %factor_ref.1), calls=%async_computation | async-start | bytes 262144 | tf_op jit(solution)/shard_map/all_to_all | solution.py:318
  10.6 6.9 %all-to-all-done = bf16[8,2,32,128]{3,2,1,0:T(8,128)(2,1)S(1)} async-done(((bf16[8,2,32,128]{3,2,1,0:T(8,128)(2,1)}), bf16[8,2,32,128]{3,2,1,0:T(8,128)(2,1)S(1)}, u32[]{:S(2)}, u32[]{:S(2)}) %all-to-all-start) | async-done | bytes 131104 | tf_op jit(solution)/shard_map/all_to_all | solution.py:318
  17.5 0.0 copy-start.2
  17.5 0.0 copy-start.3
  17.5 0.0 copy-start.4
  17.5 0.9 %copy-done.2 = bf16[8,2,32,128]{3,2,1,0:T(8,128)(2,1)S(1)} copy-done((bf16[8,2,32,128]{3,2,1,0:T(8,128)(2,1)S(1)}, bf16[8,2,32,128]{3,2,1,0:T(8,128)(2,1)}, u32[]{:S(2)}) %copy-start.2) | copy-done | bytes 131096
  18.4 0.1 copy-done.3
  18.5 0.0 copy-done.4
  18.5 0.0 copy-start
  18.5 1.2 %copy-done = bf16[1024,512]{1,0:T(8,128)(2,1)S(1)} copy-done((bf16[1024,512]{1,0:T(8,128)(2,1)S(1)}, bf16[1024,512]{1,0:T(8,128)(2,1)}, u32[]{:S(2)}) %copy-start) | copy-done | bytes 1048600
  19.7 0.0 copy-start.1
  19.7 1.2 %copy-done.1 = bf16[512,1024]{1,0:T(8,128)(2,1)S(1)} copy-done((bf16[512,1024]{1,0:T(8,128)(2,1)S(1)}, bf16[512,1024]{1,0:T(8,128)(2,1)}, u32[]{:S(2)}) %copy-start.1) | copy-done | bytes 1048600
  20.9 36.2 %shard_map.64 = f32[8,2,32,128]{3,2,1,0:T(8,128)S(1)} custom-call(bf16[8,2,32,128]{3,2,1,0:T(8,128)(2,1)S(1)} %copy-done.2, bf16[8,2,32,128]{3,2,1,0:T(8,128)(2,1)S(1)} %copy-done.3, bf16[2,2,128,128]{3,2,1,0:T(8,128)(2,1)S(1)} %bitcast.6, f32[8]{0:T(128)S(1)} %copy-done.4, s32[1]{0:T(128)S(6)} %copy.9.cutoff_ref, bf16[512,1024]{1,0:T(8,128)(2,1)S(1)} %copy-done.1, ...), custom_call_target="tpu_custom_call" | custom-call | tf_op jit(solution)/shard_map/pallas_call | solution.py:323
  57.1 0.7 %copy.10 = f32[8,2,128,32]{2,3,1,0:T(8,128)} copy(f32[8,2,128,32]{2,3,1,0:T(8,128)S(1)} %bitcast.5) | data formatting | bytes 524288
  (1 shorter events, 0.0 us)
Async XLA Ops:
  0.0 17.5 %all-to-all-start = ((bf16[8,2,32,128]{3,2,1,0:T(8,128)(2,1)}), bf16[8,2,32,128]{3,2,1,0:T(8,128)(2,1)S(1)}, u32[]{:S(2)}, u32[]{:S(2)}) async-start(bf16[8,2,32,128]{3,2,1,0:T(8,128)(2,1)} %factor_ref.1), calls=%async_computation | async-start | bytes 262144 | tf_op jit(solution)/shard_map/all_to_all | solution.py:318
  17.5 0.9 %copy-start.2 = (bf16[8,2,32,128]{3,2,1,0:T(8,128)(2,1)S(1)}, bf16[8,2,32,128]{3,2,1,0:T(8,128)(2,1)}, u32[]{:S(2)}) copy-start(bf16[8,2,32,128]{3,2,1,0:T(8,128)(2,1)} %factor_ref.1) | copy-start | bytes 393220
  17.5 1.0 %copy-start.3 = (bf16[8,2,32,128]{3,2,1,0:T(8,128)(2,1)S(1)}, bf16[8,2,32,128]{3,2,1,0:T(8,128)(2,1)}, u32[]{:S(2)}) copy-start(bf16[8,2,32,128]{3,2,1,0:T(8,128)(2,1)} %spectrum_ref.1) | copy-start | bytes 393220
  17.5 1.0 %copy-start.4 = (f32[8]{0:T(128)S(1)}, f32[8]{0:T(128)}, u32[]{:S(2)}) copy-start(f32[8]{0:T(128)} %scale_ref.1) | copy-start | bytes 100
  18.5 1.2 %copy-start = (bf16[1024,512]{1,0:T(8,128)(2,1)S(1)}, bf16[1024,512]{1,0:T(8,128)(2,1)}, u32[]{:S(2)}) copy-start(bf16[1024,512]{1,0:T(8,128)(2,1)} %constant.5.clone.to_freq_hbm) | copy-start | bytes 3145732
  19.7 1.2 %copy-start.1 = (bf16[512,1024]{1,0:T(8,128)(2,1)S(1)}, bf16[512,1024]{1,0:T(8,128)(2,1)}, u32[]{:S(2)}) copy-start(bf16[512,1024]{1,0:T(8,128)(2,1)} %constant.4.clone.to_lag_hbm) | copy-start | bytes 3145732
where the time goes:
time: 58.1 us; the launch traced here: 57.8 us
  Pallas kernels  36.2 us (62%)
  starting transfers between devices  9.95 us (17%)
  waiting for transfers between devices  6.92 us (12%)
  local copies, waits for them, and re-layouts  4.11 us (7%)
  between operations  0.68 us (1%)
    pallas_call x1, Pallas kernels, step(): pl.pallas_call(kernel, out_shape=jax.ShapeDtypeStruct((FL, 2, PANEL, C),...  36.2 us
    all_to_all x1, starting transfers between devices, step(): lax.all_to_all(factor, 'chan', split_axis=0, concat_axis=2, tiled=True)  9.95 us
    all_to_all x1, waiting for transfers between devices, step(): lax.all_to_all(factor, 'chan', split_axis=0, concat_axis=2, tiled=True)  6.92 us
    unnamed x11, local copies, waits for them, and re-layouts  4.1 us
  transfers between devices with their start and end apart: 1, of which 1 were waited for; matrix products, arithmetic and copies ran while one was open for 0% of the time, Pallas kernels for 0%

commit v1 on v0

v1 whole, which is shorter than its diff:
```python
import functools

import jax
import jax.numpy as jnp
import numpy as np
from jax import lax
from jax.experimental import pallas as pl
from jax.experimental.pallas import tpu as pltpu
from jax.sharding import PartitionSpec as P

ITERS = 8
LOGICAL = pl.DeviceIdType.LOGICAL
BF = jnp.bfloat16
F32 = jnp.float32
C = 128
PANEL = 32
FL = 8
OWN = 2
G = 64
F = 512
LAGS = 256
VMEM_LIMIT = 67043328 - 1024 * 1024
Z_ORDER = (4, 3, 5, 2, 6, 1, 7, 0)
XY_ORDER = (2, 1, 3, 0)


def rem(a, b):
    return lax.rem(a, jnp.int32(b))


def div(a, b):
    return lax.div(a, jnp.int32(b))


def coords():
    f = lax.axis_index("freq")
    c = lax.axis_index("chan")
    return div(f, 16), rem(f, 4), div(c, 2) * 4 + rem(div(f, 4), 4), rem(c, 2)


def split(value):
    high = value.astype(BF)
    return high, (value - high.astype(F32)).astype(BF)


def embed(value):
    re, im = value[:, :C], value[:, C:]
    return jnp.concatenate([value, jnp.concatenate([-im, re], axis=1)], axis=0)


def dot(left, right):
    return jnp.dot(left, right, preferred_element_type=F32)


def dot_nt(left, right):
    return lax.dot_general(left, right, (((1,), (1,)), ((), ())), preferred_element_type=F32)


def dot_tn(left, right):
    return lax.dot_general(left, right, (((0,), (0,)), ((), ())), preferred_element_type=F32)


def dot_tt(left, right):
    return lax.dot_general(left, right, (((0,), (1,)), ((), ())), preferred_element_type=F32)


def tables():
    lag = np.arange(LAGS)[:, None]
    freq = np.arange(F)[None, :]
    angle = 2.0 * np.pi * ((lag * freq) % F) / F
    cos, sin = np.cos(angle), np.sin(angle)
    to_lag = np.concatenate([cos, sin], axis=1) / F
    to_freq = np.concatenate([cos.T, -sin.T], axis=1)

    def halves(table):
        high = table.astype(jnp.bfloat16)
        low = (table - high.astype(np.float64)).astype(jnp.bfloat16)
        return np.concatenate([high, low], axis=0)

    return halves(to_lag), halves(to_freq)


def turn(value, lane):
    ahead = pltpu.roll(value, 96, 1)
    behind = pltpu.roll(value, 32, 1)
    return jnp.where(rem(lane, 64) < 32, -ahead, behind)


def table_apply(table_ref, rows, value, lane):
    high, low = split(value)
    turn_high, turn_low = turn(value, lane), None
    turn_high, turn_low = split(turn_high)
    both = jnp.concatenate(
        [jnp.concatenate([high, low], axis=1), jnp.concatenate([turn_high, turn_low], axis=1)], axis=0
    )
    first = dot(table_ref[0:rows, :], both)
    second = dot(table_ref[rows : 2 * rows, :], jnp.concatenate([high, turn_high], axis=0))
    return first[:, :C] + first[:, C:] + second


def kernel(
    factor_ref, spectrum_ref, scale_ref, cutoff_ref, to_lag_hbm, to_freq_hbm, out_ref,
    spec_all, psi_all, send_f, recv_f, send_r, recv_r, to_lag, to_freq, stage_sem, local_sem, send_sem, recv_sem,
):
    x, y, z, k = coords()
    me_f = lax.axis_index("freq")
    me_c = lax.axis_index("chan")
    me_lin = me_f * 4 + me_c
    z_hi = div(z, 4)

    xs = [rem(x + i, 4) for i in range(4)]
    ys = [rem(y + i, 4) for i in range(4)]
    zs = [rem(z + i, 8) for i in range(8)]
    x_part = [v * 64 for v in xs]
    y_part = [v * 4 for v in ys]
    z_part = [rem(v, 4) * 16 + div(v, 4) * 2 for v in zs]
    k_part = [k, 1 - k]
    x_slot = [v * 16 for v in xs]
    z_slot = [rem(v, 4) * 4 + div(v, 4) * 128 for v in zs]
    k_slot = [k * 64, 64 - k * 64]

    def number(dx, dy, dz, dk):
        return x_part[dx] + y_part[dy] + z_part[dz] + k_part[dk]

    on_y = [number(0, i, 0, 0) for i in (2, 1, 3)]
    on_z = [number(0, 0, i, 0) for i in Z_ORDER[:-1]]
    on_x = [number(i, 0, 0, 0) for i in (2, 1, 3)]
    sibling, across, diagonal = number(0, 0, 0, 1), number(0, 0, 4, 0), number(0, 0, 4, 1)
    sibling_c, across_c, diagonal_c = rem(sibling, 4), rem(across, 4), rem(diagonal, 4)

    def signal(sem, peers):
        for peer in peers:
            pl.semaphore_signal(sem, inc=1, device_id=peer, device_id_type=LOGICAL)

    def remote(src, dst, i, peer):
        return pltpu.make_async_remote_copy(
            src_ref=src, dst_ref=dst, send_sem=send_sem.at[i], recv_sem=recv_sem.at[i], device_id=peer, device_id_type=LOGICAL
        )

    def wait_bytes(ref, sem):
        pltpu.make_async_copy(ref, ref, sem).wait()

    barrier = pltpu.get_barrier_semaphore()
    first_peers = [diagonal] + on_z + on_x + on_y + [sibling]
    signal(barrier, first_peers)

    def panel_rows(chan):
        return pl.ds(pl.multiple_of(chan * PANEL, PANEL), PANEL)

    def own_freqs(chan):
        return pl.ds(OWN * chan, OWN)

    my_rows = panel_rows(me_c)
    own_copies = [
        pltpu.make_async_copy(factor_ref, psi_all.at[:, :, my_rows, :], local_sem.at[0]),
        pltpu.make_async_copy(spectrum_ref.at[own_freqs(me_c)], spec_all.at[:, :, my_rows, :], local_sem.at[1]),
    ]
    tables_in = [
        pltpu.make_async_copy(to_lag_hbm, to_lag, local_sem.at[2]),
        pltpu.make_async_copy(to_freq_hbm, to_freq, local_sem.at[3]),
    ]
    for copy in own_copies + tables_in:
        copy.start()

    pl.semaphore_wait(barrier, len(first_peers))
    partners = ((across, across_c), (diagonal, diagonal_c), (sibling, sibling_c))
    for peer, chan in partners:
        freqs = own_freqs(chan)
        remote(factor_ref.at[freqs], psi_all.at[freqs, :, my_rows, :], 0, peer).start()
    for peer, chan in partners:
        remote(spectrum_ref.at[own_freqs(chan)], spec_all.at[:, :, my_rows, :], 1, peer).start()
    here_half = pl.ds(4 * z_hi, 4)
    there_half = pl.ds(4 - 4 * z_hi, 4)
    there_rows = pl.ds(pl.multiple_of(64 - 64 * z_hi, 64), 64)
    mine = own_freqs(me_c)
    later = [
        remote(factor_ref.at[here_half], psi_all.at[here_half, :, my_rows, :], 2, across),
        remote(factor_ref.at[there_half], psi_all.at[there_half, :, my_rows, :], 3, sibling),
        remote(factor_ref.at[mine], psi_all.at[mine, :, my_rows, :], 4, sibling),
    ]
    for copy in later:
        copy.start()
    signal(stage_sem.at[0], [sibling])
    pl.semaphore_wait(stage_sem.at[0], 1)
    signal(stage_sem.at[1], on_y)
    pl.semaphore_wait(stage_sem.at[1], 3)
    signal(stage_sem.at[2], on_z)

    own_copies[0].wait()
    wait_bytes(psi_all.at[pl.ds(0, OWN), :, pl.ds(0, 3 * PANEL), :], recv_sem.at[0])
    got = psi_all.at[mine, :, there_rows, :]
    relay_own = remote(got, got, 5, sibling)
    relay_own.start()

    row = lax.broadcasted_iota(jnp.int32, (C, 2 * C), 0)
    col = lax.broadcasted_iota(jnp.int32, (C, 2 * C), 1)
    eye = (row == col).astype(F32)
    lane = lax.broadcasted_iota(jnp.int32, (G, C), 1)

    psis, rs, qs = [], [], []
    for b in range(OWN):
        psi = jnp.concatenate([psi_all[OWN * me_c + b, 0], psi_all[OWN * me_c + b, 1]], axis=1)
        wide = embed(psi)
        r = eye - scale_ref[OWN * me_c + b] * dot_nt(psi, wide)
        psis.append(wide)
        rs.append(r)
        qs.append(eye + r)

    for step in range(1, ITERS):
        for b in range(OWN):
            r_high, r_low = split(rs[b])
            q_high, q_low = split(qs[b])
            square_left = jnp.concatenate([r_high, r_low, r_high], axis=1)
            e_high, e_low = embed(r_high), embed(r_low)
            right = jnp.concatenate([e_high, e_high, e_low], axis=0)
            r_next = dot(square_left, right)
            rs[b] = r_next
            n_high, n_low = split(r_next)
            en_high, en_low = embed(n_high), embed(n_low)
            qs[b] = qs[b] + dot(
                jnp.concatenate([q_high, q_low, q_high], axis=1), jnp.concatenate([en_high, en_high, en_low], axis=0)
            )

    own_copies[1].wait()
    wait_bytes(spec_all.at[:, :, pl.ds(0, 3 * PANEL), :], recv_sem.at[1])

    for b in range(OWN):
        q_high, q_low = split(qs[b])
        zz = scale_ref[OWN * me_c + b] * dot(
            jnp.concatenate([q_high, q_low], axis=1), jnp.concatenate([psis[b], psis[b]], axis=0)
        )
        z_high, z_low = split(zz)
        spec = jnp.concatenate([spec_all[b, 0], spec_all[b, 1]], axis=1)
        u = dot(
            jnp.concatenate([spec, spec], axis=1), jnp.concatenate([embed(z_high), embed(z_low)], axis=0)
        )
        u_high, u_low = split(u)

        def upright(value):
            return jnp.concatenate([value[:, :C], -value[:, C:]], axis=0)

        zs_high, zs_low = upright(z_high), upright(z_low)
        eu_high, eu_low = embed(u_high), embed(u_low)
        mid = eye + dot_tn(
            jnp.concatenate([zs_high, zs_low, zs_high], axis=0), jnp.concatenate([eu_high, eu_high, eu_low], axis=0)
        )
        pieces = [mid[:G, :C], mid[:G, C:], mid[G:, :C], mid[G:, C:]]
        for j in range(4):
            rolled = []
            for i, piece in enumerate(pieces):
                shift = (32 * i - 32 * j) % C
                rolled.append(pltpu.roll(piece, shift, 1) if shift else piece)
            packed = jnp.where(
                lane < 64,
                jnp.where(lane < 32, rolled[0], rolled[1]),
                jnp.where(lane < 96, rolled[2], rolled[3]),
            )
            send_f[pl.ds(G * j, G), b, :] = packed

    pl.semaphore_wait(stage_sem.at[2], len(on_z))
    kept = pltpu.make_async_copy(send_f.at[me_c * G + me_f], recv_f.at[me_lin], local_sem.at[4])
    kept.start()
    for dx in XY_ORDER:
        for dy in XY_ORDER:
            for dk in (1, 0):
                for dz in Z_ORDER:
                    if (dx, dy, dz, dk) != (0, 0, 0, 0):
                        slot = x_slot[dx] + ys[dy] + z_slot[dz] + k_slot[dk]
                        remote(send_f.at[slot], recv_f.at[me_lin], 6, number(dx, dy, dz, dk)).start()

    got = psi_all.at[there_half, :, panel_rows(across_c), :]
    wait_bytes(got, recv_sem.at[2])
    relay_rest = remote(got, got, 7, sibling)
    relay_rest.start()

    for copy in tables_in:
        copy.wait()
    kept.wait()
    wait_bytes(recv_f.at[pl.ds(0, 4 * G - 1)], recv_sem.at[6])

    gathered = recv_f[...].reshape(F, C)
    lane_f = lax.broadcasted_iota(jnp.int32, (F, C), 1)
    lane_l = lax.broadcasted_iota(jnp.int32, (LAGS, C), 1)
    lag_row = lax.broadcasted_iota(jnp.int32, (LAGS, C), 0)
    keep = jnp.where(lag_row == 0, 0.5, jnp.where(lag_row <= cutoff_ref[0], 1.0, 0.0)).astype(F32)
    lags = table_apply(to_lag, LAGS, gathered, lane_f) * keep
    send_r[...] = table_apply(to_freq, F, lags, lane_l)

    me_eight = pl.ds(pl.multiple_of(me_f * FL, FL), FL)
    kept = pltpu.make_async_copy(send_r.at[me_eight, :], recv_r.at[me_eight, :], local_sem.at[5])
    kept.start()
    z_lo = rem(z, 4)
    zl = [rem(z_lo + i, 4) for i in range(4)]
    for dx in XY_ORDER:
        for dy in XY_ORDER:
            for dz in (3, 1, 2, 0):
                if (dx, dy, dz) != (0, 0, 0):
                    other = x_slot[dx] + zl[dz] * 4 + ys[dy]
                    eight = pl.ds(pl.multiple_of(other * FL, FL), FL)
                    remote(send_r.at[eight, :], recv_r.at[me_eight, :], 8, other * 4 + me_c).start()

    later[1].wait_recv()
    later[2].wait_recv()
    relay_own.wait_recv()
    relay_rest.wait_recv()
    kept.wait()
    wait_bytes(recv_r.at[pl.ds(0, F - FL), :], recv_sem.at[8])

    for f in range(FL):
        d = recv_r[pl.ds(f, G, stride=FL), :]
        high, low = split(d)
        stack = jnp.concatenate(
            [
                jnp.concatenate([high[:, :64], low[:, :64]], axis=1),
                jnp.concatenate([high[:, 64:], low[:, 64:]], axis=1),
            ],
            axis=0,
        )
        both = jnp.concatenate([psi_all[f, 0], psi_all[f, 1]], axis=0)
        got = dot_tt(stack, both)
        got = got[:64] + got[64:]
        out_ref[f, 0] = got[:32, :C] - got[32:, C:]
        out_ref[f, 1] = got[32:, :C] + got[:32, C:]

    wait_bytes(psi_all.at[pl.ds(0, OWN), :, pl.ds(0, 3 * PANEL), :], send_sem.at[0])
    wait_bytes(spec_all.at[:, :, pl.ds(0, 3 * PANEL), :], send_sem.at[1])
    for copy in later + [relay_own, relay_rest]:
        copy.wait_send()
    wait_bytes(send_f.at[pl.ds(0, 4 * G - 1)], send_sem.at[6])
    wait_bytes(send_r.at[pl.ds(0, F - FL), :], send_sem.at[8])


def step(factor, spectrum, guess_scale, lag_cutoff):
    to_lag, to_freq = tables()
    vmem = pl.BlockSpec(memory_space=pltpu.VMEM)
    smem = pl.BlockSpec(memory_space=pltpu.SMEM)
    hbm = pl.BlockSpec(memory_space=pltpu.HBM)
    dma = pltpu.SemaphoreType.DMA
    out = pl.pallas_call(
        kernel,
        out_shape=jax.ShapeDtypeStruct((FL, 2, PANEL, C), F32),
        in_specs=[hbm, hbm, smem, smem, hbm, hbm],
        out_specs=vmem,
        scratch_shapes=[
            pltpu.VMEM((OWN, 2, C, C), BF),
            pltpu.VMEM((FL, 2, C, C), BF),
            pltpu.VMEM((4 * G, OWN, C), F32),
            pltpu.VMEM((4 * G, OWN, C), F32),
            pltpu.VMEM((F, C), F32),
            pltpu.VMEM((F, C), F32),
            pltpu.VMEM(to_lag.shape, BF),
            pltpu.VMEM(to_freq.shape, BF),
            pltpu.SemaphoreType.REGULAR((3,)),
            dma((6,)),
            dma((9,)),
            dma((9,)),
        ],
        compiler_params=pltpu.CompilerParams(collective_id=0, has_side_effects=True, vmem_limit_bytes=VMEM_LIMIT),
    )(factor, spectrum, guess_scale, lag_cutoff, jnp.asarray(to_lag), jnp.asarray(to_freq))
    return jnp.swapaxes(out, 2, 3)


def solution(mesh):
    in_specs = (P("freq", None, "chan", None), P("freq", None, "chan", None), P("freq"), P())
    out_specs = P("freq", None, None, "chan")
    return jax.shard_map(step, mesh=mesh, in_specs=in_specs, out_specs=out_specs, check_vma=False)
```

time: 58.1 us -> 46.1 us (0.79)
  starting transfers between devices: 9.95 us -> 0 us
  Pallas kernels: 36.2 us -> 43.7 us
  waiting for transfers between devices: 6.92 us -> 0 us
  local copies, waits for them, and re-layouts: 4.11 us -> 1.67 us
    all_to_all x1 -> x0, starting transfers between devices: 9.95 us -> none  [step(): lax.all_to_all(factor, 'chan', split_axis=0, concat_axis=2, tiled=True)]
    pallas_call x1, Pallas kernels: 36.2 us -> 43.7 us  [step(): pl.pallas_call(kernel, out_shape=jax.ShapeDtypeStruct((FL, 2, PANEL, C),...]
    all_to_all x1 -> x0, waiting for transfers between devices: 6.92 us -> none  [step(): lax.all_to_all(factor, 'chan', split_axis=0, concat_axis=2, tiled=True)]
    unnamed x11 -> x1, local copies, waits for them, and re-layouts: 4.1 us -> 1.67 us
  transfers between devices with their start and end apart: 1 -> 0, of which waited for: 1 -> 0; matrix products, arithmetic and copies ran while one was open for 0% -> 0% of each run, Pallas kernels for 0% -> 0%
where the time goes in v1:
time: 46.1 us; the launch traced here: 46 us
  Pallas kernels  43.7 us (95%)
  local copies, waits for them, and re-layouts  1.67 us (4%)
  between operations  0.66 us (1%)
    pallas_call x1, Pallas kernels, step(): pl.pallas_call(kernel, out_shape=jax.ShapeDtypeStruct((FL, 2, PANEL, C),...  43.7 us
    unnamed x1, local copies, waits for them, and re-layouts  1.67 us

profile of v1, /device:TPU:1, one launch (start us, length us, event | category | flops | bytes accessed | tf_op | source)
XLA Modules:
  0.0 46.0 jit_solution(2142197425746451688)
XLA Ops:
  0.7 43.7 %shard_map.64 = f32[8,2,32,128]{3,2,1,0:T(8,128)} custom-call(bf16[8,2,32,128]{3,2,1,0:T(8,128)(2,1)} %factor_ref.1, bf16[8,2,32,128]{3,2,1,0:T(8,128)(2,1)} %spectrum_ref.1, f32[8]{0:T(128)} %scale_ref.1, s32[1]{0:T(128)S(6)} %copy.8.cutoff_ref, bf16[512,1024]{1,0:T(8,128)(2,1)} %constant.4.clone.to_lag_hbm, bf16[1024,512]{1,0:T(8,128)(2,1)} %constant.5.clone.to_freq_hbm), custom_call_target="tpu_custom_call" | custom-call | tf_op jit(solution)/shard_map/pallas_call | solution.py:339
  44.3 1.7 %copy.9 = f32[8,2,128,32]{2,3,1,0:T(8,128)} copy(f32[8,2,128,32]{2,3,1,0:T(8,128)} %bitcast.1) | data formatting | bytes 524288

commit v2 on v1

--- a/solution.py
+++ b/solution.py
@@ -1,4 +1,4 @@
-import functools
+import math
 
 import jax
 import jax.numpy as jnp
@@ -19,6 +19,8 @@
 G = 64
 F = 512
 LAGS = 256
+FLOOR = 2.0**-16
+STEPS = 32767 / (40 * math.log(2.0))
 VMEM_LIMIT = 67043328 - 1024 * 1024
 Z_ORDER = (4, 3, 5, 2, 6, 1, 7, 0)
 XY_ORDER = (2, 1, 3, 0)
@@ -48,6 +50,26 @@
     return jnp.concatenate([value, jnp.concatenate([-im, re], axis=1)], axis=0)
 
 
+def code(value):
+    steps = jnp.minimum(jnp.log(1.0 + jnp.abs(value) * (1.0 / FLOOR)) * STEPS + 0.5, 32767.0).astype(jnp.int32)
+    return jnp.where(value < 0, -steps, steps)
+
+
+def decode(number):
+    value = number.astype(F32)
+    size = FLOOR * jnp.exp(jnp.abs(value) * (1.0 / STEPS)) - FLOOR
+    return jnp.where(number < 0, -size, size)
+
+
+def pack(low, high):
+    return code(low) + (code(high) << 16)
+
+
+def unpack(word):
+    low = (word << 16) >> 16
+    return decode(low), decode((word - low) >> 16)
+
+
 def dot(left, right):
     return jnp.dot(left, right, preferred_element_type=F32)
 
@@ -65,58 +87,68 @@
 
 
 def tables():
-    lag = np.arange(LAGS)[:, None]
-    freq = np.arange(F)[None, :]
-    angle = 2.0 * np.pi * ((lag * freq) % F) / F
-    cos, sin = np.cos(angle), np.sin(angle)
-    to_lag = np.concatenate([cos, sin], axis=1) / F
-    to_freq = np.concatenate([cos.T, -sin.T], axis=1)
-
-    def halves(table):
-        high = table.astype(jnp.bfloat16)
-        low = (table - high.astype(np.float64)).astype(jnp.bfloat16)
-        return np.concatenate([high, low], axis=0)
-
-    return halves(to_lag), halves(to_freq)
-
-
-def turn(value, lane):
-    ahead = pltpu.roll(value, 96, 1)
-    behind = pltpu.roll(value, 32, 1)
-    return jnp.where(rem(lane, 64) < 32, -ahead, behind)
-
-
-def table_apply(table_ref, rows, value, lane):
+    to_lag, to_freq = [], []
+    pairs = np.arange(C).reshape(C // 2, 2).T.reshape(-1)
+    fours = np.arange(C).reshape(C // 8, 2, 4).swapaxes(0, 1).reshape(-1)
+    for r in range(4):
+        lag = 4 * np.arange(LAGS // 4) + r
+        angle = 2.0 * np.pi * (np.outer(lag, pairs) % F) / F
+        to_lag.append(np.concatenate([np.cos(angle), np.sin(angle)], axis=0) / F)
+        angle = 2.0 * np.pi * (np.outer(lag, fours) % F) / F
+        to_freq.append(np.concatenate([np.cos(angle).T, -np.sin(angle).T], axis=1))
+    table = np.concatenate(to_lag + to_freq, axis=0)
+    high = table.astype(jnp.bfloat16)
+    low = (table - high.astype(np.float64)).astype(jnp.bfloat16)
+    return np.concatenate([high, low], axis=0)
+
+
+def turn(value):
+    lane = lax.broadcasted_iota(jnp.int32, value.shape, 1)
+    return jnp.where(rem(lane, 64) < 32, -pltpu.roll(value, 96, 1), pltpu.roll(value, 32, 1))
+
+
+def table_dot(table_ref, block, value):
     high, low = split(value)
-    turn_high, turn_low = turn(value, lane), None
-    turn_high, turn_low = split(turn_high)
-    both = jnp.concatenate(
-        [jnp.concatenate([high, low], axis=1), jnp.concatenate([turn_high, turn_low], axis=1)], axis=0
-    )
-    first = dot(table_ref[0:rows, :], both)
-    second = dot(table_ref[rows : 2 * rows, :], jnp.concatenate([high, turn_high], axis=0))
-    return first[:, :C] + first[:, C:] + second
+    first = dot(table_ref[pl.ds(C * block, C), :], jnp.concatenate([high, low], axis=1))
+    return first[:, :C] + first[:, C:] + dot(table_ref[pl.ds(C * (block + 8), C), :], high)
+
+
+def project(table_ref, m, cutoff):
+    even, odd, even_d, odd_d = m[0] + m[2], m[1] + m[3], m[0] - m[2], turn(m[1] - m[3])
+    sums = [even + odd, even_d + odd_d, even - odd, even_d - odd_d]
+    row = lax.broadcasted_iota(jnp.int32, (LAGS // 4, C), 0)
+    back = []
+    for r in range(4):
+        both = table_dot(table_ref, r, sums[r])
+        lag = 4 * row + r
+        keep = jnp.where(lag == 0, 0.5, jnp.where(lag <= cutoff, 1.0, 0.0)).astype(F32)
+        lags = (both[: LAGS // 4] + turn(both[LAGS // 4 :])) * keep
+        back.append(table_dot(table_ref, 4 + r, jnp.concatenate([lags, turn(lags)], axis=0)))
+    even, odd, even_d, odd_d = back[0] + back[2], back[1] + back[3], back[0] - back[2], turn(back[1] - back[3])
+    return [even + odd, even_d - odd_d, even - odd, even_d + odd_d]
 
 
 def kernel(
-    factor_ref, spectrum_ref, scale_ref, cutoff_ref, to_lag_hbm, to_freq_hbm, out_ref,
-    spec_all, psi_all, send_f, recv_f, send_r, recv_r, to_lag, to_freq, stage_sem, local_sem, send_sem, recv_sem,
+    factor_ref, spectrum_ref, scale_hbm, cutoff_ref, table_hbm, out_ref,
+    spec_all, psi_all, send_f, recv_f, send_r, recv_r, table, scale_ref, stage_sem, local_sem, send_sem, recv_sem,
 ):
     x, y, z, k = coords()
     me_f = lax.axis_index("freq")
     me_c = lax.axis_index("chan")
     me_lin = me_f * 4 + me_c
-    z_hi = div(z, 4)
-
-    xs = [rem(x + i, 4) for i in range(4)]
-    ys = [rem(y + i, 4) for i in range(4)]
-    zs = [rem(z + i, 8) for i in range(8)]
+    z_hi = div(me_c, 2)
+
+    def wrapped(value, size):
+        return [value] + [value + i - jnp.where(value >= size - i, size, 0) for i in range(1, size)]
+
+    xs, ys, zs = wrapped(x, 4), wrapped(y, 4), wrapped(z, 8)
+    zh = [jnp.where(v >= 4, 1, 0) for v in zs]
     x_part = [v * 64 for v in xs]
     y_part = [v * 4 for v in ys]
-    z_part = [rem(v, 4) * 16 + div(v, 4) * 2 for v in zs]
+    z_part = [v * 16 - h * 62 for v, h in zip(zs, zh)]
     k_part = [k, 1 - k]
     x_slot = [v * 16 for v in xs]
-    z_slot = [rem(v, 4) * 4 + div(v, 4) * 128 for v in zs]
+    z_slot = [v * 4 + h * 112 for v, h in zip(zs, zh)]
     k_slot = [k * 64, 64 - k * 64]
 
     def number(dx, dy, dz, dk):
@@ -126,7 +158,9 @@
     on_z = [number(0, 0, i, 0) for i in Z_ORDER[:-1]]
     on_x = [number(i, 0, 0, 0) for i in (2, 1, 3)]
     sibling, across, diagonal = number(0, 0, 0, 1), number(0, 0, 4, 0), number(0, 0, 4, 1)
-    sibling_c, across_c, diagonal_c = rem(sibling, 4), rem(across, 4), rem(diagonal, 4)
+    sibling_c = 2 * z_hi + 1 - k
+    across_c = 2 - 2 * z_hi + k
+    diagonal_c = 3 - 2 * z_hi - k
 
     def signal(sem, peers):
         for peer in peers:
@@ -155,11 +189,9 @@
         pltpu.make_async_copy(factor_ref, psi_all.at[:, :, my_rows, :], local_sem.at[0]),
         pltpu.make_async_copy(spectrum_ref.at[own_freqs(me_c)], spec_all.at[:, :, my_rows, :], local_sem.at[1]),
     ]
-    tables_in = [
-        pltpu.make_async_copy(to_lag_hbm, to_lag, local_sem.at[2]),
-        pltpu.make_async_copy(to_freq_hbm, to_freq, local_sem.at[3]),
-    ]
-    for copy in own_copies + tables_in:
+    scale_in = pltpu.make_async_copy(scale_hbm, scale_ref, local_sem.at[2])
+    table_in = pltpu.make_async_copy(table_hbm, table, local_sem.at[3])
+    for copy in own_copies + [scale_in, table_in]:
         copy.start()
 
     pl.semaphore_wait(barrier, len(first_peers))
@@ -187,6 +219,7 @@
     signal(stage_sem.at[2], on_z)
 
     own_copies[0].wait()
+    scale_in.wait()
     wait_bytes(psi_all.at[pl.ds(0, OWN), :, pl.ds(0, 3 * PANEL), :], recv_sem.at[0])
     got = psi_all.at[mine, :, there_rows, :]
     relay_own = remote(got, got, 5, sibling)
@@ -224,38 +257,44 @@
     own_copies[1].wait()
     wait_bytes(spec_all.at[:, :, pl.ds(0, 3 * PANEL), :], recv_sem.at[1])
 
+    def upright(value):
+        return jnp.concatenate([value[:, :C], -value[:, C:]], axis=0)
+
+    specs = [jnp.concatenate([spec_all[b, 0], spec_all[b, 1]], axis=1) for b in range(OWN)]
+    zs_split, us_split = [], []
     for b in range(OWN):
         q_high, q_low = split(qs[b])
-        zz = scale_ref[OWN * me_c + b] * dot(
-            jnp.concatenate([q_high, q_low], axis=1), jnp.concatenate([psis[b], psis[b]], axis=0)
-        )
-        z_high, z_low = split(zz)
-        spec = jnp.concatenate([spec_all[b, 0], spec_all[b, 1]], axis=1)
+        zz = dot(jnp.concatenate([q_high, q_low], axis=1), jnp.concatenate([psis[b], psis[b]], axis=0))
+        zs_split.append(split(scale_ref[OWN * me_c + b] * zz))
+    for b in range(OWN):
+        z_high, z_low = zs_split[b]
         u = dot(
-            jnp.concatenate([spec, spec], axis=1), jnp.concatenate([embed(z_high), embed(z_low)], axis=0)
-        )
-        u_high, u_low = split(u)
-
-        def upright(value):
-            return jnp.concatenate([value[:, :C], -value[:, C:]], axis=0)
-
-        zs_high, zs_low = upright(z_high), upright(z_low)
-        eu_high, eu_low = embed(u_high), embed(u_low)
-        mid = eye + dot_tn(
-            jnp.concatenate([zs_high, zs_low, zs_high], axis=0), jnp.concatenate([eu_high, eu_high, eu_low], axis=0)
-        )
-        pieces = [mid[:G, :C], mid[:G, C:], mid[G:, :C], mid[G:, C:]]
-        for j in range(4):
-            rolled = []
-            for i, piece in enumerate(pieces):
-                shift = (32 * i - 32 * j) % C
-                rolled.append(pltpu.roll(piece, shift, 1) if shift else piece)
-            packed = jnp.where(
-                lane < 64,
-                jnp.where(lane < 32, rolled[0], rolled[1]),
-                jnp.where(lane < 96, rolled[2], rolled[3]),
+            jnp.concatenate([specs[b], specs[b]], axis=1), jnp.concatenate([embed(z_high), embed(z_low)], axis=0)
+        )
+        us_split.append(split(u))
+    mids = []
+    for b in range(OWN):
+        zs_high, zs_low = upright(zs_split[b][0]), upright(zs_split[b][1])
+        eu_high, eu_low = embed(us_split[b][0]), embed(us_split[b][1])
+        mids.append(
+            eye
+            + dot_tn(
+                jnp.concatenate([zs_high, zs_low, zs_high], axis=0), jnp.concatenate([eu_high, eu_high, eu_low], axis=0)
             )
-            send_f[pl.ds(G * j, G), b, :] = packed
+        )
+    half = C // 2
+    words = [pack(mids[0][:, :C], mids[1][:, :C]), pack(mids[0][:, C:], mids[1][:, C:])]
+    pieces = [words[0][:half], words[1][:half], words[0][half:], words[1][half:]]
+    for j in range(4):
+        rolled = []
+        for i, piece in enumerate(pieces):
+            shift = (32 * i - 32 * j) % C
+            rolled.append(pltpu.roll(piece, shift, 1) if shift else piece)
+        send_f[pl.ds(G * j, G), 0, :] = jnp.where(
+            lane < 64,
+            jnp.where(lane < 32, rolled[0], rolled[1]),
+            jnp.where(lane < 96, rolled[2], rolled[3]),
+        )
 
     pl.semaphore_wait(stage_sem.at[2], len(on_z))
     kept = pltpu.make_async_copy(send_f.at[me_c * G + me_f], recv_f.at[me_lin], local_sem.at[4])
@@ -273,42 +312,36 @@
     relay_rest = remote(got, got, 7, sibling)
     relay_rest.start()
 
-    for copy in tables_in:
-        copy.wait()
+    table_in.wait()
     kept.wait()
     wait_bytes(recv_f.at[pl.ds(0, 4 * G - 1)], recv_sem.at[6])
 
-    gathered = recv_f[...].reshape(F, C)
-    lane_f = lax.broadcasted_iota(jnp.int32, (F, C), 1)
-    lane_l = lax.broadcasted_iota(jnp.int32, (LAGS, C), 1)
-    lag_row = lax.broadcasted_iota(jnp.int32, (LAGS, C), 0)
-    keep = jnp.where(lag_row == 0, 0.5, jnp.where(lag_row <= cutoff_ref[0], 1.0, 0.0)).astype(F32)
-    lags = table_apply(to_lag, LAGS, gathered, lane_f) * keep
-    send_r[...] = table_apply(to_freq, F, lags, lane_l)
-
-    me_eight = pl.ds(pl.multiple_of(me_f * FL, FL), FL)
-    kept = pltpu.make_async_copy(send_r.at[me_eight, :], recv_r.at[me_eight, :], local_sem.at[5])
+    even, odd = unpack(recv_f[...].reshape(4 * G, C))
+    blocks = [jnp.concatenate([even[G * i : G * (i + 1)], odd[G * i : G * (i + 1)]], axis=0) for i in range(4)]
+    parts = project(table, blocks, cutoff_ref[0])
+    for i in range(4):
+        send_r[pl.ds(G // 4 * i, G // 4)] = pack(parts[i][:G], parts[i][G:]).reshape(G // 4, 4, C)
+
+    kept = pltpu.make_async_copy(send_r.at[me_f], recv_r.at[me_f], local_sem.at[5])
     kept.start()
-    z_lo = rem(z, 4)
-    zl = [rem(z_lo + i, 4) for i in range(4)]
+    zl = wrapped(z - 4 * z_hi, 4)
     for dx in XY_ORDER:
         for dy in XY_ORDER:
             for dz in (3, 1, 2, 0):
                 if (dx, dy, dz) != (0, 0, 0):
                     other = x_slot[dx] + zl[dz] * 4 + ys[dy]
-                    eight = pl.ds(pl.multiple_of(other * FL, FL), FL)
-                    remote(send_r.at[eight, :], recv_r.at[me_eight, :], 8, other * 4 + me_c).start()
+                    remote(send_r.at[other], recv_r.at[me_f], 8, other * 4 + me_c).start()
 
     later[1].wait_recv()
     later[2].wait_recv()
     relay_own.wait_recv()
     relay_rest.wait_recv()
     kept.wait()
-    wait_bytes(recv_r.at[pl.ds(0, F - FL), :], recv_sem.at[8])
-
+    wait_bytes(recv_r.at[pl.ds(0, G - 1)], recv_sem.at[8])
+
+    causal = [unpack(recv_r[:, f, :]) for f in range(4)]
     for f in range(FL):
-        d = recv_r[pl.ds(f, G, stride=FL), :]
-        high, low = split(d)
+        high, low = split(causal[f % 4][f // 4])
         stack = jnp.concatenate(
             [
                 jnp.concatenate([high[:, :64], low[:, :64]], axis=1),
@@ -327,11 +360,11 @@
     for copy in later + [relay_own, relay_rest]:
         copy.wait_send()
     wait_bytes(send_f.at[pl.ds(0, 4 * G - 1)], send_sem.at[6])
-    wait_bytes(send_r.at[pl.ds(0, F - FL), :], send_sem.at[8])
+    wait_bytes(send_r.at[pl.ds(0, G - 1)], send_sem.at[8])
 
 
 def step(factor, spectrum, guess_scale, lag_cutoff):
-    to_lag, to_freq = tables()
+    table = tables()
     vmem = pl.BlockSpec(memory_space=pltpu.VMEM)
     smem = pl.BlockSpec(memory_space=pltpu.SMEM)
     hbm = pl.BlockSpec(memory_space=pltpu.HBM)
@@ -339,24 +372,24 @@
     out = pl.pallas_call(
         kernel,
         out_shape=jax.ShapeDtypeStruct((FL, 2, PANEL, C), F32),
-        in_specs=[hbm, hbm, smem, smem, hbm, hbm],
+        in_specs=[hbm, hbm, hbm, smem, hbm],
         out_specs=vmem,
         scratch_shapes=[
             pltpu.VMEM((OWN, 2, C, C), BF),
             pltpu.VMEM((FL, 2, C, C), BF),
-            pltpu.VMEM((4 * G, OWN, C), F32),
-            pltpu.VMEM((4 * G, OWN, C), F32),
-            pltpu.VMEM((F, C), F32),
-            pltpu.VMEM((F, C), F32),
-            pltpu.VMEM(to_lag.shape, BF),
-            pltpu.VMEM(to_freq.shape, BF),
+            pltpu.VMEM((4 * G, 1, C), jnp.int32),
+            pltpu.VMEM((4 * G, 1, C), jnp.int32),
+            pltpu.VMEM((G, 4, C), jnp.int32),
+            pltpu.VMEM((G, 4, C), jnp.int32),
+            pltpu.VMEM(table.shape, BF),
+            pltpu.SMEM((FL,), F32),
             pltpu.SemaphoreType.REGULAR((3,)),
             dma((6,)),
             dma((9,)),
             dma((9,)),
         ],
         compiler_params=pltpu.CompilerParams(collective_id=0, has_side_effects=True, vmem_limit_bytes=VMEM_LIMIT),
-    )(factor, spectrum, guess_scale, lag_cutoff, jnp.asarray(to_lag), jnp.asarray(to_freq))
+    )(factor, spectrum, guess_scale, lag_cutoff, jnp.asarray(table))
     return jnp.swapaxes(out, 2, 3)
 
 

time: 46.1 us -> 44.1 us (0.957)
  Pallas kernels: 43.7 us -> 41.7 us
    pallas_call x1, Pallas kernels: 43.7 us -> 41.7 us  [step(): pl.pallas_call(kernel, out_shape=jax.ShapeDtypeStruct((FL, 2, PANEL, C),...]
where the time goes in v2:
time: 44.1 us; the launch traced here: 44 us
  Pallas kernels  41.7 us (95%)
  local copies, waits for them, and re-layouts  1.67 us (4%)
  between operations  0.66 us (1%)
    pallas_call x1, Pallas kernels, step(): pl.pallas_call(kernel, out_shape=jax.ShapeDtypeStruct((FL, 2, PANEL, C),...  41.7 us
    unnamed x1, local copies, waits for them, and re-layouts  1.67 us

profile of v2, /device:TPU:1, one launch (start us, length us, event | category | flops | bytes accessed | tf_op | source)
XLA Modules:
  0.0 44.0 jit_solution(14422631006506985387)
XLA Ops:
  0.7 41.7 %shard_map.55 = f32[8,2,32,128]{3,2,1,0:T(8,128)} custom-call(bf16[8,2,32,128]{3,2,1,0:T(8,128)(2,1)} %factor_ref.1, bf16[8,2,32,128]{3,2,1,0:T(8,128)(2,1)} %spectrum_ref.1, f32[8]{0:T(128)} %scale_hbm.1, s32[1]{0:T(128)S(6)} %copy.7.cutoff_ref, bf16[2048,128]{1,0:T(8,128)(2,1)} %constant.2.clone.table_hbm), custom_call_target="tpu_custom_call" | custom-call | tf_op jit(solution)/shard_map/pallas_call | solution.py:372
  42.3 1.7 %copy.8 = f32[8,2,128,32]{2,3,1,0:T(8,128)} copy(f32[8,2,128,32]{2,3,1,0:T(8,128)} %bitcast.1) | data formatting | bytes 524288

commit v3 on v2

--- a/solution.py
+++ b/solution.py
@@ -21,7 +21,7 @@
 LAGS = 256
 FLOOR = 2.0**-16
 STEPS = 32767 / (40 * math.log(2.0))
-VMEM_LIMIT = 67043328 - 1024 * 1024
+VMEM_LIMIT = 67043328 - 11000 * 1024
 Z_ORDER = (4, 3, 5, 2, 6, 1, 7, 0)
 XY_ORDER = (2, 1, 3, 0)
 
@@ -147,9 +147,6 @@
     y_part = [v * 4 for v in ys]
     z_part = [v * 16 - h * 62 for v, h in zip(zs, zh)]
     k_part = [k, 1 - k]
-    x_slot = [v * 16 for v in xs]
-    z_slot = [v * 4 + h * 112 for v, h in zip(zs, zh)]
-    k_slot = [k * 64, 64 - k * 64]
 
     def number(dx, dy, dz, dk):
         return x_part[dx] + y_part[dy] + z_part[dz] + k_part[dk]
@@ -201,10 +198,9 @@
         remote(factor_ref.at[freqs], psi_all.at[freqs, :, my_rows, :], 0, peer).start()
     for peer, chan in partners:
         remote(spectrum_ref.at[own_freqs(chan)], spec_all.at[:, :, my_rows, :], 1, peer).start()
+    mine = own_freqs(me_c)
     here_half = pl.ds(4 * z_hi, 4)
     there_half = pl.ds(4 - 4 * z_hi, 4)
-    there_rows = pl.ds(pl.multiple_of(64 - 64 * z_hi, 64), 64)
-    mine = own_freqs(me_c)
     later = [
         remote(factor_ref.at[here_half], psi_all.at[here_half, :, my_rows, :], 2, across),
         remote(factor_ref.at[there_half], psi_all.at[there_half, :, my_rows, :], 3, sibling),
@@ -212,6 +208,7 @@
     ]
     for copy in later:
         copy.start()
+
     signal(stage_sem.at[0], [sibling])
     pl.semaphore_wait(stage_sem.at[0], 1)
     signal(stage_sem.at[1], on_y)
@@ -221,6 +218,7 @@
     own_copies[0].wait()
     scale_in.wait()
     wait_bytes(psi_all.at[pl.ds(0, OWN), :, pl.ds(0, 3 * PANEL), :], recv_sem.at[0])
+    there_rows = pl.ds(pl.multiple_of(64 - 64 * z_hi, 64), 64)
     got = psi_all.at[mine, :, there_rows, :]
     relay_own = remote(got, got, 5, sibling)
     relay_own.start()
@@ -239,37 +237,40 @@
         rs.append(r)
         qs.append(eye + r)
 
-    for step in range(1, ITERS):
+    def times(left, right_high, right_low):
+        high, low = split(left)
+        e_high, e_low = embed(right_high), embed(right_low)
+        rows = left.shape[0]
+        most = dot(jnp.concatenate([high, low], axis=0), e_high)
+        return most[:rows] + (most[rows:] + dot(high, e_low))
+
+    for step in range(ITERS):
         for b in range(OWN):
-            r_high, r_low = split(rs[b])
-            q_high, q_low = split(qs[b])
-            square_left = jnp.concatenate([r_high, r_low, r_high], axis=1)
-            e_high, e_low = embed(r_high), embed(r_low)
-            right = jnp.concatenate([e_high, e_high, e_low], axis=0)
-            r_next = dot(square_left, right)
-            rs[b] = r_next
-            n_high, n_low = split(r_next)
-            en_high, en_low = embed(n_high), embed(n_low)
-            qs[b] = qs[b] + dot(
-                jnp.concatenate([q_high, q_low, q_high], axis=1), jnp.concatenate([en_high, en_high, en_low], axis=0)
-            )
-
-    own_copies[1].wait()
-    wait_bytes(spec_all.at[:, :, pl.ds(0, 3 * PANEL), :], recv_sem.at[1])
+            right = split(rs[b])
+            if step == 0:
+                rs[b] = times(rs[b], *right)
+            elif step < ITERS - 1:
+                both = times(jnp.concatenate([rs[b], qs[b]], axis=0), *right)
+                rs[b] = both[:C]
+                qs[b] = qs[b] + both[C:]
+            else:
+                qs[b] = qs[b] + times(qs[b], *right)
 
     def upright(value):
         return jnp.concatenate([value[:, :C], -value[:, C:]], axis=0)
 
-    specs = [jnp.concatenate([spec_all[b, 0], spec_all[b, 1]], axis=1) for b in range(OWN)]
     zs_split, us_split = [], []
     for b in range(OWN):
         q_high, q_low = split(qs[b])
-        zz = dot(jnp.concatenate([q_high, q_low], axis=1), jnp.concatenate([psis[b], psis[b]], axis=0))
-        zs_split.append(split(scale_ref[OWN * me_c + b] * zz))
+        zz = dot(jnp.concatenate([q_high, q_low], axis=0), psis[b])
+        zs_split.append(split(scale_ref[OWN * me_c + b] * (zz[:C] + zz[C:])))
+    own_copies[1].wait()
+    wait_bytes(spec_all.at[:, :, pl.ds(0, 3 * PANEL), :], recv_sem.at[1])
     for b in range(OWN):
         z_high, z_low = zs_split[b]
+        spec = jnp.concatenate([spec_all[b, 0], spec_all[b, 1]], axis=1)
         u = dot(
-            jnp.concatenate([specs[b], specs[b]], axis=1), jnp.concatenate([embed(z_high), embed(z_low)], axis=0)
+            jnp.concatenate([spec, spec], axis=1), jnp.concatenate([embed(z_high), embed(z_low)], axis=0)
         )
         us_split.append(split(u))
     mids = []
@@ -290,14 +291,17 @@
         for i, piece in enumerate(pieces):
             shift = (32 * i - 32 * j) % C
             rolled.append(pltpu.roll(piece, shift, 1) if shift else piece)
-        send_f[pl.ds(G * j, G), 0, :] = jnp.where(
+        send_f[pl.ds(G * j, G), :] = jnp.where(
             lane < 64,
             jnp.where(lane < 32, rolled[0], rolled[1]),
             jnp.where(lane < 96, rolled[2], rolled[3]),
         )
 
+    x_slot = [v * 16 for v in xs]
+    z_slot = [v * 4 + h * 112 for v, h in zip(zs, zh)]
+    k_slot = [k * 64, 64 - k * 64]
     pl.semaphore_wait(stage_sem.at[2], len(on_z))
-    kept = pltpu.make_async_copy(send_f.at[me_c * G + me_f], recv_f.at[me_lin], local_sem.at[4])
+    kept = pltpu.make_async_copy(send_f.at[pl.ds(me_c * G + me_f, 1)], recv_f.at[pl.ds(me_lin, 1)], local_sem.at[4])
     kept.start()
     for dx in XY_ORDER:
         for dy in XY_ORDER:
@@ -305,7 +309,7 @@
                 for dz in Z_ORDER:
                     if (dx, dy, dz, dk) != (0, 0, 0, 0):
                         slot = x_slot[dx] + ys[dy] + z_slot[dz] + k_slot[dk]
-                        remote(send_f.at[slot], recv_f.at[me_lin], 6, number(dx, dy, dz, dk)).start()
+                        remote(send_f.at[pl.ds(slot, 1)], recv_f.at[pl.ds(me_lin, 1)], 6, number(dx, dy, dz, dk)).start()
 
     got = psi_all.at[there_half, :, panel_rows(across_c), :]
     wait_bytes(got, recv_sem.at[2])
@@ -316,13 +320,14 @@
     kept.wait()
     wait_bytes(recv_f.at[pl.ds(0, 4 * G - 1)], recv_sem.at[6])
 
-    even, odd = unpack(recv_f[...].reshape(4 * G, C))
+    even, odd = unpack(recv_f[...])
     blocks = [jnp.concatenate([even[G * i : G * (i + 1)], odd[G * i : G * (i + 1)]], axis=0) for i in range(4)]
     parts = project(table, blocks, cutoff_ref[0])
     for i in range(4):
-        send_r[pl.ds(G // 4 * i, G // 4)] = pack(parts[i][:G], parts[i][G:]).reshape(G // 4, 4, C)
-
-    kept = pltpu.make_async_copy(send_r.at[me_f], recv_r.at[me_f], local_sem.at[5])
+        send_r[pl.ds(G * i, G), :] = pack(parts[i][:G], parts[i][G:])
+
+    me_four = pl.ds(pl.multiple_of(me_f * 4, 4), 4)
+    kept = pltpu.make_async_copy(send_r.at[me_four], recv_r.at[me_four], local_sem.at[5])
     kept.start()
     zl = wrapped(z - 4 * z_hi, 4)
     for dx in XY_ORDER:
@@ -330,16 +335,17 @@
             for dz in (3, 1, 2, 0):
                 if (dx, dy, dz) != (0, 0, 0):
                     other = x_slot[dx] + zl[dz] * 4 + ys[dy]
-                    remote(send_r.at[other], recv_r.at[me_f], 8, other * 4 + me_c).start()
+                    four = pl.ds(pl.multiple_of(other * 4, 4), 4)
+                    remote(send_r.at[four], recv_r.at[me_four], 8, other * 4 + me_c).start()
 
     later[1].wait_recv()
     later[2].wait_recv()
     relay_own.wait_recv()
     relay_rest.wait_recv()
     kept.wait()
-    wait_bytes(recv_r.at[pl.ds(0, G - 1)], recv_sem.at[8])
-
-    causal = [unpack(recv_r[:, f, :]) for f in range(4)]
+    wait_bytes(recv_r.at[pl.ds(0, 4 * G - 4)], recv_sem.at[8])
+
+    causal = [unpack(recv_r[pl.ds(f, G, stride=4), :]) for f in range(4)]
     for f in range(FL):
         high, low = split(causal[f % 4][f // 4])
         stack = jnp.concatenate(
@@ -360,7 +366,7 @@
     for copy in later + [relay_own, relay_rest]:
         copy.wait_send()
     wait_bytes(send_f.at[pl.ds(0, 4 * G - 1)], send_sem.at[6])
-    wait_bytes(send_r.at[pl.ds(0, G - 1)], send_sem.at[8])
+    wait_bytes(send_r.at[pl.ds(0, 4 * G - 4)], send_sem.at[8])
 
 
 def step(factor, spectrum, guess_scale, lag_cutoff):
@@ -377,10 +383,10 @@
         scratch_shapes=[
             pltpu.VMEM((OWN, 2, C, C), BF),
             pltpu.VMEM((FL, 2, C, C), BF),
-            pltpu.VMEM((4 * G, 1, C), jnp.int32),
-            pltpu.VMEM((4 * G, 1, C), jnp.int32),
-            pltpu.VMEM((G, 4, C), jnp.int32),
-            pltpu.VMEM((G, 4, C), jnp.int32),
+            pltpu.VMEM((4 * G, C), jnp.int32),
+            pltpu.VMEM((4 * G, C), jnp.int32),
+            pltpu.VMEM((4 * G, C), jnp.int32),
+            pltpu.VMEM((4 * G, C), jnp.int32),
             pltpu.VMEM(table.shape, BF),
             pltpu.SMEM((FL,), F32),
             pltpu.SemaphoreType.REGULAR((3,)),

time: 44.1 us -> 41.5 us (0.941)
  Pallas kernels: 41.7 us -> 38.2 us
  local copies, waits for them, and re-layouts: 1.67 us -> 2.51 us
    pallas_call x1, Pallas kernels: 41.7 us -> 38.2 us  [step(): pl.pallas_call(kernel, out_shape=jax.ShapeDtypeStruct((FL, 2, PANEL, C),...]
    unnamed x1 -> x7, local copies, waits for them, and re-layouts: 1.67 us -> 2.51 us
where the time goes in v3:
time: 41.5 us; the launch traced here: 41.4 us
  Pallas kernels  38.2 us (92%)
  local copies, waits for them, and re-layouts  2.51 us (6%)
  between operations  0.69 us (2%)
    pallas_call x1, Pallas kernels, step(): pl.pallas_call(kernel, out_shape=jax.ShapeDtypeStruct((FL, 2, PANEL, C),...  38.2 us
    unnamed x7, local copies, waits for them, and re-layouts  2.51 us

profile of v3, /device:TPU:1, one launch (start us, length us, event | category | flops | bytes accessed | tf_op | source)
XLA Modules:
  0.0 41.4 jit_solution(15708279912505593076)
XLA Ops:
  0.0 0.0 copy-start.2
  0.7 0.0 copy-done.2
  0.7 0.0 copy-start
  0.7 0.9 %copy-done = bf16[8,2,32,128]{3,2,1,0:T(8,128)(2,1)S(1)} copy-done((bf16[8,2,32,128]{3,2,1,0:T(8,128)(2,1)S(1)}, bf16[8,2,32,128]{3,2,1,0:T(8,128)(2,1)}, u32[]{:S(2)}) %copy-start) | copy-done | bytes 131096
  1.6 0.0 copy-start.1
  1.6 0.9 %copy-done.1 = bf16[8,2,32,128]{3,2,1,0:T(8,128)(2,1)S(1)} copy-done((bf16[8,2,32,128]{3,2,1,0:T(8,128)(2,1)S(1)}, bf16[8,2,32,128]{3,2,1,0:T(8,128)(2,1)}, u32[]{:S(2)}) %copy-start.1) | copy-done | bytes 131096
  2.5 38.2 %shard_map.55 = f32[8,2,32,128]{3,2,1,0:T(8,128)S(1)} custom-call(bf16[8,2,32,128]{3,2,1,0:T(8,128)(2,1)S(1)} %copy-done, bf16[8,2,32,128]{3,2,1,0:T(8,128)(2,1)S(1)} %copy-done.1, f32[8]{0:T(128)S(1)} %copy-done.2, s32[1]{0:T(128)S(6)} %copy.7.cutoff_ref, bf16[2048,128]{1,0:T(8,128)(2,1)} %constant.2.clone.table_hbm), custom_call_target="tpu_custom_call" | custom-call | tf_op jit(solution)/shard_map/pallas_call | solution.py:378
  40.7 0.7 %copy.8 = f32[8,2,128,32]{2,3,1,0:T(8,128)} copy(f32[8,2,128,32]{2,3,1,0:T(8,128)S(1)} %bitcast.1) | data formatting | bytes 524288
Async XLA Ops:
  0.0 0.7 %copy-start.2 = (f32[8]{0:T(128)S(1)}, f32[8]{0:T(128)}, u32[]{:S(2)}) copy-start(f32[8]{0:T(128)} %scale_hbm.1) | copy-start | bytes 100
  0.7 0.9 %copy-start = (bf16[8,2,32,128]{3,2,1,0:T(8,128)(2,1)S(1)}, bf16[8,2,32,128]{3,2,1,0:T(8,128)(2,1)}, u32[]{:S(2)}) copy-start(bf16[8,2,32,128]{3,2,1,0:T(8,128)(2,1)} %factor_ref.1) | copy-start | bytes 393220
  1.6 0.9 %copy-start.1 = (bf16[8,2,32,128]{3,2,1,0:T(8,128)(2,1)S(1)}, bf16[8,2,32,128]{3,2,1,0:T(8,128)(2,1)}, u32[]{:S(2)}) copy-start(bf16[8,2,32,128]{3,2,1,0:T(8,128)(2,1)} %spectrum_ref.1) | copy-start | bytes 393220

commit v4 on v3

--- a/solution.py
+++ b/solution.py
@@ -21,7 +21,7 @@
 LAGS = 256
 FLOOR = 2.0**-16
 STEPS = 32767 / (40 * math.log(2.0))
-VMEM_LIMIT = 67043328 - 11000 * 1024
+VMEM_LIMIT = 67043328 - 10500 * 1024
 Z_ORDER = (4, 3, 5, 2, 6, 1, 7, 0)
 XY_ORDER = (2, 1, 3, 0)
 
@@ -129,7 +129,7 @@
 
 
 def kernel(
-    factor_ref, spectrum_ref, scale_hbm, cutoff_ref, table_hbm, out_ref,
+    factor_ref, spectrum_ref, scale_hbm, cutoff_ref, table_hbm, out_0, out_1, out_2, out_3,
     spec_all, psi_all, send_f, recv_f, send_r, recv_r, table, scale_ref, stage_sem, local_sem, send_sem, recv_sem,
 ):
     x, y, z, k = coords()
@@ -346,7 +346,9 @@
     wait_bytes(recv_r.at[pl.ds(0, 4 * G - 4)], recv_sem.at[8])
 
     causal = [unpack(recv_r[pl.ds(f, G, stride=4), :]) for f in range(4)]
+    outs = (out_0, out_1, out_2, out_3)
     for f in range(FL):
+        out_ref = outs[f // 2]
         high, low = split(causal[f % 4][f // 4])
         stack = jnp.concatenate(
             [
@@ -358,8 +360,8 @@
         both = jnp.concatenate([psi_all[f, 0], psi_all[f, 1]], axis=0)
         got = dot_tt(stack, both)
         got = got[:64] + got[64:]
-        out_ref[f, 0] = got[:32, :C] - got[32:, C:]
-        out_ref[f, 1] = got[32:, :C] + got[:32, C:]
+        out_ref[f % 2, 0] = got[:32, :C] - got[32:, C:]
+        out_ref[f % 2, 1] = got[32:, :C] + got[:32, C:]
 
     wait_bytes(psi_all.at[pl.ds(0, OWN), :, pl.ds(0, 3 * PANEL), :], send_sem.at[0])
     wait_bytes(spec_all.at[:, :, pl.ds(0, 3 * PANEL), :], send_sem.at[1])
@@ -375,11 +377,11 @@
     smem = pl.BlockSpec(memory_space=pltpu.SMEM)
     hbm = pl.BlockSpec(memory_space=pltpu.HBM)
     dma = pltpu.SemaphoreType.DMA
-    out = pl.pallas_call(
+    outs = pl.pallas_call(
         kernel,
-        out_shape=jax.ShapeDtypeStruct((FL, 2, PANEL, C), F32),
+        out_shape=[jax.ShapeDtypeStruct((2, 2, PANEL, C), F32)] * 4,
         in_specs=[hbm, hbm, hbm, smem, hbm],
-        out_specs=vmem,
+        out_specs=[vmem] * 4,
         scratch_shapes=[
             pltpu.VMEM((OWN, 2, C, C), BF),
             pltpu.VMEM((FL, 2, C, C), BF),
@@ -396,7 +398,7 @@
         ],
         compiler_params=pltpu.CompilerParams(collective_id=0, has_side_effects=True, vmem_limit_bytes=VMEM_LIMIT),
     )(factor, spectrum, guess_scale, lag_cutoff, jnp.asarray(table))
-    return jnp.swapaxes(out, 2, 3)
+    return jnp.swapaxes(jnp.concatenate(outs, axis=0), 2, 3)
 
 
 def solution(mesh):

time: 41.5 us -> 40.1 us (0.966)
  local copies, waits for them, and re-layouts: 2.51 us -> 0.01 us
  other arithmetic: 0 us -> 0.72 us
    unnamed x7 -> x2, local copies, waits for them, and re-layouts: 2.51 us -> 0.01 us
    transpose x0 -> x1, other arithmetic: none -> 0.72 us  [step(): return jnp.swapaxes(jnp.concatenate(outs, axis=0), 2, 3)]
    pallas_call x1, Pallas kernels: 38.2 us -> 38.6 us  [step(): pl.pallas_call(kernel, out_shape=[jax.ShapeDtypeStruct((2, 2, PANEL, C),...]
where the time goes in v4:
time: 40.1 us; the launch traced here: 40 us
  Pallas kernels  38.6 us (96%)
  other arithmetic  0.72 us (2%)
  between operations  0.68 us (2%)
    pallas_call x1, Pallas kernels, step(): pl.pallas_call(kernel, out_shape=[jax.ShapeDtypeStruct((2, 2, PANEL, C),...  38.6 us

profile of v4, /device:TPU:1, one launch (start us, length us, event | category | flops | bytes accessed | tf_op | source)
XLA Modules:
  0.0 40.0 jit_solution(6930326383178383365)
XLA Ops:
  0.0 0.0 copy-start
  0.7 0.0 copy-done
  0.7 38.6 %shard_map.55 = (f32[2,2,32,128]{3,2,1,0:T(8,128)S(1)}, f32[2,2,32,128]{3,2,1,0:T(8,128)S(1)}, f32[2,2,32,128]{3,2,1,0:T(8,128)S(1)}, f32[2,2,32,128]{3,2,1,0:T(8,128)S(1)}) custom-call(bf16[8,2,32,128]{3,2,1,0:T(8,128)(2,1)} %factor_ref.1, bf16[8,2,32,128]{3,2,1,0:T(8,128)(2,1)} %spectrum_ref.1, f32[8]{0:T(128)S(1)} %copy-done, s32[1]{0:T(128)S(6)} %copy.6.cutoff_ref, ...), custom_call_target="tpu_custom_call" | custom-call | tf_op jit(solution)/shard_map/pallas_call | solution.py:380
  39.3 0.7 %maximum_bitcast_fusion = f32[8,2,128,32]{2,3,1,0:T(8,128)} fusion(f32[2,2,32,128]{3,2,1,0:T(8,128)S(1)} %get-tuple-element.12, f32[2,2,32,128]{3,2,1,0:T(8,128)S(1)} %get-tuple-element.11, f32[2,2,32,128]{3,2,1,0:T(8,128)S(1)} %get-tuple-element.10, f32[2,2,32,128]{3,2,1,0:T(8,128)S(1)} %get-tuple-element.9), kind=kLoop, calls=%fused_computation | loop fusion | flops 196608 | bytes 524288 | tf_op jit(solution)/shard_map/transpose | solution.py:401
Async XLA Ops:
  0.0 0.7 %copy-start = (f32[8]{0:T(128)S(1)}, f32[8]{0:T(128)}, u32[]{:S(2)}) copy-start(f32[8]{0:T(128)} %scale_hbm.1) | copy-start | bytes 100

commit v5 on v4

--- a/solution.py
+++ b/solution.py
@@ -1,5 +1,3 @@
-import math
-
 import jax
 import jax.numpy as jnp
 import numpy as np
@@ -20,7 +18,7 @@
 F = 512
 LAGS = 256
 FLOOR = 2.0**-16
-STEPS = 32767 / (40 * math.log(2.0))
+STEPS = 32767 / 40
 VMEM_LIMIT = 67043328 - 10500 * 1024
 Z_ORDER = (4, 3, 5, 2, 6, 1, 7, 0)
 XY_ORDER = (2, 1, 3, 0)
@@ -51,13 +49,13 @@
 
 
 def code(value):
-    steps = jnp.minimum(jnp.log(1.0 + jnp.abs(value) * (1.0 / FLOOR)) * STEPS + 0.5, 32767.0).astype(jnp.int32)
+    steps = jnp.minimum(jnp.log2(1.0 + jnp.abs(value) * (1.0 / FLOOR)) * STEPS + 0.5, 32767.0).astype(jnp.int32)
     return jnp.where(value < 0, -steps, steps)
 
 
 def decode(number):
     value = number.astype(F32)
-    size = FLOOR * jnp.exp(jnp.abs(value) * (1.0 / STEPS)) - FLOOR
+    size = jnp.exp2(jnp.abs(value) * (1.0 / STEPS) - 16.0) - FLOOR
     return jnp.where(number < 0, -size, size)
 
 
@@ -130,7 +128,7 @@
 
 def kernel(
     factor_ref, spectrum_ref, scale_hbm, cutoff_ref, table_hbm, out_0, out_1, out_2, out_3,
-    spec_all, psi_all, send_f, recv_f, send_r, recv_r, table, scale_ref, stage_sem, local_sem, send_sem, recv_sem,
+    spec_all, psi_all, send_f, recv_f, part_all, send_r, recv_r, table, scale_ref, stage_sem, local_sem, send_sem, recv_sem,
 ):
     x, y, z, k = coords()
     me_f = lax.axis_index("freq")
@@ -324,13 +322,13 @@
     blocks = [jnp.concatenate([even[G * i : G * (i + 1)], odd[G * i : G * (i + 1)]], axis=0) for i in range(4)]
     parts = project(table, blocks, cutoff_ref[0])
     for i in range(4):
-        send_r[pl.ds(G * i, G), :] = pack(parts[i][:G], parts[i][G:])
+        part_all[i] = parts[i]
 
     me_four = pl.ds(pl.multiple_of(me_f * 4, 4), 4)
-    kept = pltpu.make_async_copy(send_r.at[me_four], recv_r.at[me_four], local_sem.at[5])
-    kept.start()
     zl = wrapped(z - 4 * z_hi, 4)
     for dx in XY_ORDER:
+        part = part_all[xs[dx]]
+        send_r[pl.ds(pl.multiple_of(xs[dx] * G, G), G), :] = pack(part[:G], part[G:])
         for dy in XY_ORDER:
             for dz in (3, 1, 2, 0):
                 if (dx, dy, dz) != (0, 0, 0):
@@ -338,6 +336,8 @@
                     four = pl.ds(pl.multiple_of(other * 4, 4), 4)
                     remote(send_r.at[four], recv_r.at[me_four], 8, other * 4 + me_c).start()
 
+    kept = pltpu.make_async_copy(send_r.at[me_four], recv_r.at[me_four], local_sem.at[5])
+    kept.start()
     later[1].wait_recv()
     later[2].wait_recv()
     relay_own.wait_recv()
@@ -387,6 +387,7 @@
             pltpu.VMEM((FL, 2, C, C), BF),
             pltpu.VMEM((4 * G, C), jnp.int32),
             pltpu.VMEM((4 * G, C), jnp.int32),
+            pltpu.VMEM((4, C, C), F32),
             pltpu.VMEM((4 * G, C), jnp.int32),
             pltpu.VMEM((4 * G, C), jnp.int32),
             pltpu.VMEM(table.shape, BF),

time: 40.1 us -> 40 us (level)
  no operation moved by 1% of the time
where the time goes in v5:
time: 40 us
  Pallas kernels  38.6 us (96%)
  other arithmetic  0.72 us (2%)
  between operations  0.68 us (2%)
    pallas_call x1, Pallas kernels, step(): pl.pallas_call(kernel, out_shape=[jax.ShapeDtypeStruct((2, 2, PANEL, C),...  38.6 us

profile of v5, /device:TPU:1, one launch (start us, length us, event | category | flops | bytes accessed | tf_op | source)
XLA Modules:
  0.0 40.0 jit_solution(9095213607376999777)
XLA Ops:
  0.0 0.0 copy-start
  0.7 0.0 copy-done
  0.7 38.6 %shard_map.55 = (f32[2,2,32,128]{3,2,1,0:T(8,128)S(1)}, f32[2,2,32,128]{3,2,1,0:T(8,128)S(1)}, f32[2,2,32,128]{3,2,1,0:T(8,128)S(1)}, f32[2,2,32,128]{3,2,1,0:T(8,128)S(1)}) custom-call(bf16[8,2,32,128]{3,2,1,0:T(8,128)(2,1)} %factor_ref.1, bf16[8,2,32,128]{3,2,1,0:T(8,128)(2,1)} %spectrum_ref.1, f32[8]{0:T(128)S(1)} %copy-done, s32[1]{0:T(128)S(6)} %copy.6.cutoff_ref, ...), custom_call_target="tpu_custom_call" | custom-call | tf_op jit(solution)/shard_map/pallas_call | solution.py:380
  39.2 0.7 %maximum_bitcast_fusion = f32[8,2,128,32]{2,3,1,0:T(8,128)} fusion(f32[2,2,32,128]{3,2,1,0:T(8,128)S(1)} %get-tuple-element.12, f32[2,2,32,128]{3,2,1,0:T(8,128)S(1)} %get-tuple-element.11, f32[2,2,32,128]{3,2,1,0:T(8,128)S(1)} %get-tuple-element.10, f32[2,2,32,128]{3,2,1,0:T(8,128)S(1)} %get-tuple-element.9), kind=kLoop, calls=%fused_computation | loop fusion | flops 196608 | bytes 524288 | tf_op jit(solution)/shard_map/transpose | solution.py:402
Async XLA Ops:
  0.0 0.7 %copy-start = (f32[8]{0:T(128)S(1)}, f32[8]{0:T(128)}, u32[]{:S(2)}) copy-start(f32[8]{0:T(128)} %scale_hbm.1) | copy-start | bytes 100
